TPU v7x, 32 devices: a whole 2x2x4 slice. The times are simulated.
32 devices in a mesh: req: 8 (over z, x), tp: 4 (over y, core).
Axes of the slice: x: 2, y: 2, z: 4, core: 2. Of those that a mesh axis runs over, the one named last changes fastest.
Arguments:
- hidden: bfloat16 [512, 2048], P('req')
- norm_gain: float32 [2048], replicated, may hold values from 0.5 to 1.5
- head_weight: bfloat16 [2048, 12288], P(None, ('req', 'tp'))
- targets: int32 [512], P('req'), may hold values from 0 to 12287
- pad_mask: int32 [512], P('req'), may hold values 0 or 1
Outputs:
- logprob: float32 [512], P('req')
- entropy: float32 [512], P('req')
All inputs are finite; a program needn't handle non-finite values. No bound on the sum of `pad_mask` on one device may be relied on, other than what follows from the above.
Results may differ from a plain program's by a relative error of at most 0.0012.
Values may be sent and summed in bfloat16 or wider, within the bound.
A program may use at most 128 MiB of HBM per device.

v0:
```python
import jax
import jax.numpy as jnp
from jax import lax
from jax.sharding import PartitionSpec as P


def combined_all(value, axis, join):
    pieces = jax.tree.map(lambda part: lax.all_gather(part, axis), value)
    head = jax.tree.map(lambda part: part[0], pieces)
    tail = jax.tree.map(lambda part: part[1:], pieces)
    subtotal, _ = lax.scan(lambda subtotal, slab: (join(subtotal, slab), None), head, tail)
    return subtotal


def combine_stats(earlier, later):
    top_a, total_a, weighted_a, picked_a = earlier
    top_b, total_b, weighted_b, picked_b = later
    top_new = jnp.maximum(top_a, top_b)
    scale_a = jnp.exp(top_a - top_new)
    scale_b = jnp.exp(top_b - top_new)
    return (
        top_new,
        total_a * scale_a + total_b * scale_b,
        weighted_a * scale_a + weighted_b * scale_b,
        picked_a + picked_b,
    )


def body(hidden, norm_gain, head_weight, targets, pad_mask):
    slots = hidden.shape[0]
    voc_local = head_weight.shape[1]
    tp_count = lax.axis_size("tp")
    voc_start = (lax.axis_index("req") * tp_count + lax.axis_index("tp")) * voc_local
    wide = hidden.astype(jnp.float32)
    scale = lax.rsqrt(jnp.mean(wide * wide, axis=1, keepdims=True) + 1e-05)
    normed = (wide * scale * norm_gain[None, :]).astype(jnp.bfloat16)
    columns = lax.broadcasted_iota(jnp.int32, (1, voc_local), 1)
    all_targets = lax.all_gather(targets, "req", axis=0, tiled=True)
    logits = jnp.dot(
        lax.all_gather(normed, "req", axis=0, tiled=True),
        head_weight,
        preferred_element_type=jnp.float32,
    )
    top_row = jnp.max(logits, axis=1)
    expo = jnp.exp(logits - top_row[:, None])
    local = all_targets - voc_start
    picked_row = jnp.sum(jnp.where(columns == local[:, None], logits, jnp.float32(0.0)), axis=1)
    parts = (top_row, jnp.sum(expo, axis=1), jnp.sum(expo * logits, axis=1), picked_row)
    stats = tuple((fresh for fresh in parts))
    merged = combined_all(stats, ("req", "tp"), combine_stats)
    own_start = lax.axis_index("req") * slots
    top_all, total_all, weighted_all, picked_all = tuple(
        (lax.dynamic_slice_in_dim(whole, own_start, slots, 0) for whole in merged)
    )
    lse = top_all + jnp.log(total_all)
    live = pad_mask.astype(jnp.float32)
    logprob = (picked_all - lse) * live
    entropy = (lse - weighted_all / total_all) * live
    return (logprob, entropy)


def solution(mesh):
    return jax.shard_map(
        body,
        mesh=mesh,
        in_specs=(P("req", None), P(), P(None, ("req", "tp")), P("req"), P("req")),
        out_specs=(P("req"), P("req")),
        check_vma=False,
    )
```

profile of v0, /device:TPU:0, one launch (start us, length us, event | category | flops | bytes accessed | tf_op | source)
XLA Modules:
  0.0 227.5 jit_solution(6988182918797164582)
XLA Ops:
  7.2 0.0 copy-start
  7.2 0.0 all-gather.10.cloned.1.call-start
  7.2 1.2 fusion.1
  8.5 1.8 fusion.3
  10.3 0.0 all-gather.10.cloned.1.call-update
  10.3 1.2 dynamic-slice
  12.2 0.9 dynamic-update-slice
  13.1 13.1 %all-reduce = s32[512]{0:T(512)S(1)} all-reduce(s32[512]{0:T(512)S(1)} %dynamic-update-slice), channel_id=1, replica_groups=mesh['req'=8,'tp'=4] {'req'}, use_global_device_ids=true, to_apply=%add | all-reduce | flops 512 | bytes 4096
  26.2 36.2 %all-gather.10.cloned.1.call-done = bf16[512,2048]{1,0:T(8,128)(2,1)} async-done(((bf16[64,2048]{1,0:T(8,128)(2,1)}), bf16[512,2048]{1,0:T(8,128)(2,1)}) %all-gather.10.cloned.1.call-update) | async-done | bytes 2097168 | tf_op jit(solution)/shard_map/all_gather | solution.py:40
  62.4 0.0 copy-done
  62.4 2.6 %fusion.4 = (f32[512]{0:T(512)S(1)}, f32[512,384]{0,1:T(8,128)S(1)}) fusion(bf16[512,2048]{1,0:T(8,128)(2,1)} %all-gather.10.cloned.1.call-done, bf16[2048,384]{1,0:T(8,128)(2,1)S(1)} %copy-done), kind=kOutput, calls=%fused_computation.27 | convolution fusion | flops 805502464 | bytes 4458496 | tf_op jit(solution)/shard_map/dot_general | solution.py:39
  65.1 0.0 copy-start.1
  65.1 39.2 %all-gather.4 = f32[32,1,512]{2,1,0:T(1,128)S(1)} all-gather(f32[1,1,512]{2,1,0:T(1,128)S(1)} %bitcast.49), channel_id=2, replica_groups=mesh['req'=8,'tp'=4] {'req','tp'}, dimensions={0}, use_global_device_ids=true | all-gather | bytes 67584 | tf_op jit(solution)/shard_map/all_gather | solution.py:8
  104.3 0.3 multiply_reduce_fusion
  104.5 36.8 %all-gather.5 = f32[32,1,512]{2,1,0:T(1,128)S(1)} all-gather(f32[1,1,512]{2,1,0:T(1,128)S(1)} %bitcast.51), channel_id=3, replica_groups=mesh['req'=8,'tp'=4] {'req','tp'}, dimensions={0}, use_global_device_ids=true | all-gather | bytes 67584 | tf_op jit(solution)/shard_map/all_gather | solution.py:8
  141.3 38.1 %all-gather.6 = f32[32,1,512]{2,1,0:T(1,128)S(1)} all-gather(f32[1,1,512]{2,1,0:T(1,128)S(1)} %bitcast.50), channel_id=4, replica_groups=mesh['req'=8,'tp'=4] {'req','tp'}, dimensions={0}, use_global_device_ids=true | all-gather | bytes 67584 | tf_op jit(solution)/shard_map/all_gather | solution.py:8
  179.5 36.8 %all-gather.7 = f32[32,1,512]{2,1,0:T(1,128)S(1)} all-gather(f32[1,1,512]{2,1,0:T(1,128)S(1)} %bitcast.48), channel_id=5, replica_groups=mesh['req'=8,'tp'=4] {'req','tp'}, dimensions={0}, use_global_device_ids=true | all-gather | bytes 67584 | tf_op jit(solution)/shard_map/all_gather | solution.py:8
  216.4 3.6 %while.16 = (s32[]{:T(128)}, f32[512]{0:T(512)S(1)}, f32[512]{0:T(512)S(1)}, f32[512]{0:T(512)S(1)}, f32[512]{0:T(512)S(1)}, /*index=5*/f32[31,512]{1,0:T(8,128)...) while((s32[]{:T(128)}, f32[512]{0:T(512)S(1)}, f32[512]{0:T(512)S(1)}, ...), condition=%wide.region_6.7_spmd, body=%wide.region_5.6_spmd.sunk | while | flops 6146 | bytes 51317 | solution.py:11
  220.0 0.0 copy-done.1
  220.0 0.6 subtract_multiply_fusion
  (201 shorter events, 2.3 us)
Async XLA Ops:
  7.2 55.3 %copy-start = (bf16[2048,384]{1,0:T(8,128)(2,1)S(1)}, bf16[2048,384]{1,0:T(8,128)(2,1)}, u32[]{:S(2)}) copy-start(bf16[2048,384]{1,0:T(8,128)(2,1)} %param.9) | copy-start | bytes 4718596
  7.2 55.2 %all-gather.10.cloned.1.call-start = ((), (), s32[]{:S(2)}) async-start(), calls=%async_computation | async-start | bytes 2359296 | tf_op jit(solution)/shard_map/all_gather | solution.py:40
  65.1 154.9 %copy-start.1 = (s32[64]{0:T(128)S(1)}, s32[64]{0:T(128)}, u32[]{:S(2)}) copy-start(s32[64]{0:T(128)} %param.11) | copy-start | bytes 772
Sparse Core Ops, SparseCore 0:
  10.4 51.9 all-gather.9
where the time goes:
time: 228 us; the launch traced here: 227 us
  blocking collectives  164 us (72%)
  waiting for transfers between devices  36.3 us (16%)
  between operations  14.8 us (6%)
  other arithmetic  5.27 us (2%)
  local copies, waits for them, and re-layouts  3.05 us (1%)
  matrix products  2.63 us (1%)
    all_gather x4, blocking collectives, combined_all(): pieces = jax.tree.map(lambda part: lax.all_gather(part, axis), value)  151 us
    all_gather x1, waiting for transfers between devices, body(): lax.all_gather(normed, 'req', axis=0, tiled=True)  36.2 us
    unnamed x1, blocking collectives  13.1 us
  transfers between devices with their start and end apart: 1, of which 1 were waited for; matrix products, arithmetic and copies ran while one was open for 1% of the time, Pallas kernels for 0%

commit v1 on v0

--- a/solution.py
+++ b/solution.py
@@ -2,6 +2,24 @@
 import jax.numpy as jnp
 from jax import lax
 from jax.sharding import PartitionSpec as P
+
+
+def gather_around(array, axis, dim):
+    ways, here, lap = (lax.axis_size(axis), lax.axis_index(axis), array.shape[dim])
+    shape = [n * ways if d == dim else n for d, n in enumerate(array.shape)]
+    full = lax.dynamic_update_slice_in_dim(
+        jnp.zeros(shape, array.dtype), array, here * lap, axis=dim
+    )
+    going_up = going_down = array
+    for far in range(1, ways // 2 + 1):
+        going_up = lax.ppermute(going_up, axis, [(d, (d + 1) % ways) for d in range(ways)])
+        full = lax.dynamic_update_slice_in_dim(full, going_up, (here - far) % ways * lap, axis=dim)
+        if 2 * far < ways:
+            going_down = lax.ppermute(going_down, axis, [(d, (d - 1) % ways) for d in range(ways)])
+            full = lax.dynamic_update_slice_in_dim(
+                full, going_down, (here + far) % ways * lap, axis=dim
+            )
+    return full
 
 
 def combined_all(value, axis, join):
@@ -37,9 +55,7 @@
     columns = lax.broadcasted_iota(jnp.int32, (1, voc_local), 1)
     all_targets = lax.all_gather(targets, "req", axis=0, tiled=True)
     logits = jnp.dot(
-        lax.all_gather(normed, "req", axis=0, tiled=True),
-        head_weight,
-        preferred_element_type=jnp.float32,
+        gather_around(normed, "req", 0), head_weight, preferred_element_type=jnp.float32
     )
     top_row = jnp.max(logits, axis=1)
     expo = jnp.exp(logits - top_row[:, None])

time: 228 us -> 218 us (0.956)
  waiting for transfers between devices: 36.3 us -> 11.2 us
  starting transfers between devices: 0.04 us -> 20.5 us
  between operations: 14.8 us -> 1.44 us
  local copies, waits for them, and re-layouts: 3.05 us -> 8.42 us
  blocking collectives: 164 us -> 168 us
    all_gather x1 -> x0, waiting for transfers between devices: 36.2 us -> none  [body(): lax.all_gather(normed, 'req', axis=0, tiled=True)]
    ppermute x0 -> x7, starting transfers between devices: none -> 20.5 us  [the longest x3 12.6 us: gather_around(): lax.ppermute(going_down, axis, [(d, (d - 1) % ways) for d in range(ways)])]
    ppermute x0 -> x7, waiting for transfers between devices: none -> 11.2 us  [the longest x3 7.42 us: gather_around(): lax.ppermute(going_down, axis, [(d, (d - 1) % ways) for d in range(ways)])]
    dynamic_update_slice x0 -> x7, local copies, waits for them, and re-layouts: none -> 5.02 us  [the longest x4 2.9 us: gather_around(): lax.dynamic_update_slice_in_dim(full, going_up, (here - far) % ways * lap...]
    unnamed x1, blocking collectives: 13.1 us -> 16 us
  transfers between devices with their start and end apart: 1 -> 7, of which waited for: 1 -> 2; matrix products, arithmetic and copies ran while one was open for 1% -> 2% of each run, Pallas kernels for 0% -> 0%
where the time goes in v1:
time: 218 us; the launch traced here: 217 us
  blocking collectives  168 us (77%)
  starting transfers between devices  20.5 us (9%)
  waiting for transfers between devices  11.2 us (5%)
  local copies, waits for them, and re-layouts  8.42 us (4%)
  other arithmetic  4.29 us (2%)
  matrix products  2.63 us (1%)
    all_gather x4, blocking collectives, combined_all(): pieces = jax.tree.map(lambda part: lax.all_gather(part, axis), value)  152 us
    unnamed x1, blocking collectives  16 us
    ppermute x3, starting transfers between devices, gather_around(): lax.ppermute(going_down, axis, [(d, (d - 1) % ways) for d in range(ways)])  12.6 us
    ppermute x4, starting transfers between devices, gather_around(): lax.ppermute(going_up, axis, [(d, (d + 1) % ways) for d in range(ways)])  7.94 us
    ppermute x3, waiting for transfers between devices, gather_around(): lax.ppermute(going_down, axis, [(d, (d - 1) % ways) for d in range(ways)])  7.42 us
  transfers between devices with their start and end apart: 7, of which 2 were waited for; matrix products, arithmetic and copies ran while one was open for 2% of the time, Pallas kernels for 0%

profile of v1, /device:TPU:0, one launch (start us, length us, event | category | flops | bytes accessed | tf_op | source)
XLA Modules:
  0.0 217.5 jit_solution(17901741085830032749)
XLA Ops:
  0.6 0.0 copy-start
  0.6 0.0 copy-start.5
  0.7 0.0 copy-start.1
  0.7 0.0 copy-start.2
  0.7 0.0 copy-start.4
  0.7 1.2 fusion.1
  1.9 1.6 broadcast_in_dim.5
  3.5 0.0 copy-done.1
  3.5 0.0 copy-done.2
  3.5 0.8 constant_dynamic-update-slice_fusion.7
  4.4 2.9 %collective-permute-start = (bf16[64,2048]{1,0:T(8,128)(2,1)S(1)}, bf16[64,2048]{1,0:T(8,128)(2,1)S(1)}, u32[]{:S(2)}, u32[]{:S(2)}) collective-permute-start(bf16[64,2048]{1,0:T(8,128)(2,1)S(1)} %get-tuple-element.80), channel_id=1, source_target_pairs={{0,4},{4,8},{8,12},{12,16},{16,20},{20,24},{24,28},{28,0},{1,5},{5... | collective-permute-start | bytes 786440 | tf_op jit(solution)/shard_map/ppermute | solution.py:15
  7.3 3.1 %collective-permute-start.1 = (bf16[64,2048]{1,0:T(8,128)(2,1)S(1)}, bf16[64,2048]{1,0:T(8,128)(2,1)S(1)}, u32[]{:S(2)}, u32[]{:S(2)}) collective-permute-start(bf16[64,2048]{1,0:T(8,128)(2,1)S(1)} %get-tuple-element.80), channel_id=1, source_target_pairs={{0,28},{4,0},{8,4},{12,8},{16,12},{20,16},{24,20},{28,24},{1,29},{... | collective-permute-start | bytes 786440 | tf_op jit(solution)/shard_map/ppermute | solution.py:18
  10.4 0.0 copy-done.5
  10.4 0.6 dynamic-slice
  11.6 0.0 copy-done.4
  11.6 0.2 dynamic-update-slice
  11.9 16.0 %all-reduce = s32[512]{0:T(512)S(1)} all-reduce(s32[512]{0:T(512)S(1)} %dynamic-update-slice), channel_id=1, replica_groups=mesh['req'=8,'tp'=4] {'req'}, use_global_device_ids=true, to_apply=%add | all-reduce | flops 512 | bytes 4096
  27.8 0.0 collective-permute-done
  27.8 0.6 collective-permute-start.2
  28.5 0.0 collective-permute-done.1
  28.5 4.1 %collective-permute-start.3 = (bf16[64,2048]{1,0:T(8,128)(2,1)S(1)}, bf16[64,2048]{1,0:T(8,128)(2,1)S(1)}, u32[]{:S(2)}, u32[]{:S(2)}) collective-permute-start(bf16[64,2048]{1,0:T(8,128)(2,1)S(1)} %collective-permute-done.1), channel_id=1, source_target_pairs={{0,28},{4,0},{8,4},{12,8},{16,12},{20,16},{24,20},{28,24},{1,29},{... | collective-permute-start | bytes 786440 | tf_op jit(solution)/shard_map/ppermute | solution.py:18
  32.6 0.7 constant_dynamic-update-slice_fusion.6
  33.3 0.7 constant_dynamic-update-slice_fusion.5
  34.0 3.8 %collective-permute-done.2 = bf16[64,2048]{1,0:T(8,128)(2,1)S(1)} collective-permute-done((bf16[64,2048]{1,0:T(8,128)(2,1)S(1)}, bf16[64,2048]{1,0:T(8,128)(2,1)S(1)}, u32[]{:S(2)}, u32[]{:S(2)}) %collective-permute-start.2) | collective-permute-done | bytes 262176 | tf_op jit(solution)/shard_map/ppermute | solution.py:15
  37.8 2.5 %collective-permute-start.4 = (bf16[64,2048]{1,0:T(8,128)(2,1)S(1)}, bf16[64,2048]{1,0:T(8,128)(2,1)S(1)}, u32[]{:S(2)}, u32[]{:S(2)}) collective-permute-start(bf16[64,2048]{1,0:T(8,128)(2,1)S(1)} %collective-permute-done.2), channel_id=1, source_target_pairs={{0,4},{4,8},{8,12},{12,16},{16,20},{20,24},{24,28},{28,0},{1,5},{5... | collective-permute-start | bytes 786440 | tf_op jit(solution)/shard_map/ppermute | solution.py:15
  40.3 0.0 collective-permute-done.3
  40.3 5.4 %collective-permute-start.5 = (bf16[64,2048]{1,0:T(8,128)(2,1)S(1)}, bf16[64,2048]{1,0:T(8,128)(2,1)S(1)}, u32[]{:S(2)}, u32[]{:S(2)}) collective-permute-start(bf16[64,2048]{1,0:T(8,128)(2,1)S(1)} %collective-permute-done.3), channel_id=1, source_target_pairs={{0,28},{4,0},{8,4},{12,8},{16,12},{20,16},{24,20},{28,24},{1,29},{... | collective-permute-start | bytes 786440 | tf_op jit(solution)/shard_map/ppermute | solution.py:18
  45.7 0.7 constant_dynamic-update-slice_fusion.4
  46.4 0.7 constant_dynamic-update-slice_fusion.3
  47.1 0.0 collective-permute-done.4
  47.1 1.9 collective-permute-start.6
  49.0 0.7 constant_dynamic-update-slice_fusion.2
  49.7 7.4 %collective-permute-done.5 = bf16[64,2048]{1,0:T(8,128)(2,1)S(1)} collective-permute-done((bf16[64,2048]{1,0:T(8,128)(2,1)S(1)}, bf16[64,2048]{1,0:T(8,128)(2,1)S(1)}, u32[]{:S(2)}, u32[]{:S(2)}) %collective-permute-start.5) | collective-permute-done | bytes 262176 | tf_op jit(solution)/shard_map/ppermute | solution.py:18
  57.1 0.7 constant_dynamic-update-slice_fusion.1
  57.8 0.0 collective-permute-done.6
  57.8 0.7 constant_dynamic-update-slice_fusion
  58.6 0.0 copy-done
  58.6 2.6 %fusion.5 = (f32[512]{0:T(512)S(1)}, f32[512,384]{0,1:T(8,128)S(1)}) fusion(bf16[512,2048]{1,0:T(8,128)(2,1)} %constant_dynamic-update-slice_fusion, bf16[2048,384]{1,0:T(8,128)(2,1)S(1)} %copy-done), kind=kOutput, calls=%fused_computation.35 | convolution fusion | flops 805502464 | bytes 4458496 | tf_op jit(solution)/shard_map/dot_general | solution.py:57
  61.2 0.0 copy-start.3
  61.2 0.3 multiply_reduce_fusion
  61.5 39.9 %all-gather.7 = f32[32,1,512]{2,1,0:T(1,128)S(1)} all-gather(f32[1,1,512]{2,1,0:T(1,128)S(1)} %bitcast.51), channel_id=5, replica_groups=mesh['req'=8,'tp'=4] {'req','tp'}, dimensions={0}, use_global_device_ids=true | all-gather | bytes 67584 | tf_op jit(solution)/shard_map/all_gather | solution.py:26
  101.4 36.8 %all-gather.5 = f32[32,1,512]{2,1,0:T(1,128)S(1)} all-gather(f32[1,1,512]{2,1,0:T(1,128)S(1)} %bitcast.50), channel_id=3, replica_groups=mesh['req'=8,'tp'=4] {'req','tp'}, dimensions={0}, use_global_device_ids=true | all-gather | bytes 67584 | tf_op jit(solution)/shard_map/all_gather | solution.py:26
  138.2 38.1 %all-gather.6 = f32[32,1,512]{2,1,0:T(1,128)S(1)} all-gather(f32[1,1,512]{2,1,0:T(1,128)S(1)} %bitcast.49), channel_id=4, replica_groups=mesh['req'=8,'tp'=4] {'req','tp'}, dimensions={0}, use_global_device_ids=true | all-gather | bytes 67584 | tf_op jit(solution)/shard_map/all_gather | solution.py:26
  176.3 36.8 %all-gather.4 = f32[32,1,512]{2,1,0:T(1,128)S(1)} all-gather(f32[1,1,512]{2,1,0:T(1,128)S(1)} %bitcast.48), channel_id=2, replica_groups=mesh['req'=8,'tp'=4] {'req','tp'}, dimensions={0}, use_global_device_ids=true | all-gather | bytes 67584 | tf_op jit(solution)/shard_map/all_gather | solution.py:26
  213.2 3.6 %while.16 = (s32[]{:T(128)}, f32[512]{0:T(512)S(1)}, f32[512]{0:T(512)S(1)}, f32[512]{0:T(512)S(1)}, f32[512]{0:T(512)S(1)}, /*index=5*/f32[31,512]{1,0:T(8,128)...) while((s32[]{:T(128)}, f32[512]{0:T(512)S(1)}, f32[512]{0:T(512)S(1)}, ...), condition=%wide.region_6.7_spmd, body=%wide.region_5.6_spmd.sunk | while | flops 6146 | bytes 51309 | solution.py:29
  216.9 0.0 copy-done.3
  216.9 0.6 subtract_multiply_fusion
  (201 shorter events, 2.3 us)
Async XLA Ops:
  0.6 57.9 %copy-start = (bf16[2048,384]{1,0:T(8,128)(2,1)S(1)}, bf16[2048,384]{1,0:T(8,128)(2,1)}, u32[]{:S(2)}) copy-start(bf16[2048,384]{1,0:T(8,128)(2,1)} %param.9) | copy-start | bytes 4718596
  0.6 9.7 %copy-start.5 = (u32[32]{0:T(128)S(1)}, u32[32]{0:T(128)}, u32[]{:S(2)}) copy-start(u32[32]{0:T(128)} %constant.92) | copy-start | bytes 388
  0.7 2.9 %copy-start.1 = (bf16[64,2048]{1,0:T(8,128)(2,1)S(1)}, bf16[64,2048]{1,0:T(8,128)(2,1)}, u32[]{:S(2)}) copy-start(bf16[64,2048]{1,0:T(8,128)(2,1)} %param.7) | copy-start | bytes 786436
  0.7 2.9 %copy-start.2 = (f32[2048]{0:T(1024)S(1)}, f32[2048]{0:T(1024)}, u32[]{:S(2)}) copy-start(f32[2048]{0:T(1024)} %param.8) | copy-start | bytes 24580
  0.7 10.9 %copy-start.4 = (s32[64]{0:T(128)S(1)}, s32[64]{0:T(128)}, u32[]{:S(2)}) copy-start(s32[64]{0:T(128)} %param.10) | copy-start | bytes 772
  4.4 23.5 %collective-permute-start = (bf16[64,2048]{1,0:T(8,128)(2,1)S(1)}, bf16[64,2048]{1,0:T(8,128)(2,1)S(1)}, u32[]{:S(2)}, u32[]{:S(2)}) collective-permute-start(bf16[64,2048]{1,0:T(8,128)(2,1)S(1)} %get-tuple-element.80), channel_id=1, source_target_pairs={{0,4},{4,8},{8,12},{12,16},{16,20},{20,24},{24,28},{28,0},{1,5},{5... | collective-permute-start | bytes 786440 | tf_op jit(solution)/shard_map/ppermute | solution.py:15
  7.3 21.2 %collective-permute-start.1 = (bf16[64,2048]{1,0:T(8,128)(2,1)S(1)}, bf16[64,2048]{1,0:T(8,128)(2,1)S(1)}, u32[]{:S(2)}, u32[]{:S(2)}) collective-permute-start(bf16[64,2048]{1,0:T(8,128)(2,1)S(1)} %get-tuple-element.80), channel_id=1, source_target_pairs={{0,28},{4,0},{8,4},{12,8},{16,12},{20,16},{24,20},{28,24},{1,29},{... | collective-permute-start | bytes 786440 | tf_op jit(solution)/shard_map/ppermute | solution.py:18
  27.8 10.0 %collective-permute-start.2 = (bf16[64,2048]{1,0:T(8,128)(2,1)S(1)}, bf16[64,2048]{1,0:T(8,128)(2,1)S(1)}, u32[]{:S(2)}, u32[]{:S(2)}) collective-permute-start(bf16[64,2048]{1,0:T(8,128)(2,1)S(1)} %collective-permute-done), channel_id=1, source_target_pairs={{0,4},{4,8},{8,12},{12,16},{16,20},{20,24},{24,28},{28,0},{1,5},{5... | collective-permute-start | bytes 786440 | tf_op jit(solution)/shard_map/ppermute | solution.py:15
  28.5 11.8 %collective-permute-start.3 = (bf16[64,2048]{1,0:T(8,128)(2,1)S(1)}, bf16[64,2048]{1,0:T(8,128)(2,1)S(1)}, u32[]{:S(2)}, u32[]{:S(2)}) collective-permute-start(bf16[64,2048]{1,0:T(8,128)(2,1)S(1)} %collective-permute-done.1), channel_id=1, source_target_pairs={{0,28},{4,0},{8,4},{12,8},{16,12},{20,16},{24,20},{28,24},{1,29},{... | collective-permute-start | bytes 786440 | tf_op jit(solution)/shard_map/ppermute | solution.py:18
  37.8 9.3 %collective-permute-start.4 = (bf16[64,2048]{1,0:T(8,128)(2,1)S(1)}, bf16[64,2048]{1,0:T(8,128)(2,1)S(1)}, u32[]{:S(2)}, u32[]{:S(2)}) collective-permute-start(bf16[64,2048]{1,0:T(8,128)(2,1)S(1)} %collective-permute-done.2), channel_id=1, source_target_pairs={{0,4},{4,8},{8,12},{12,16},{16,20},{20,24},{24,28},{28,0},{1,5},{5... | collective-permute-start | bytes 786440 | tf_op jit(solution)/shard_map/ppermute | solution.py:15
  40.3 16.8 %collective-permute-start.5 = (bf16[64,2048]{1,0:T(8,128)(2,1)S(1)}, bf16[64,2048]{1,0:T(8,128)(2,1)S(1)}, u32[]{:S(2)}, u32[]{:S(2)}) collective-permute-start(bf16[64,2048]{1,0:T(8,128)(2,1)S(1)} %collective-permute-done.3), channel_id=1, source_target_pairs={{0,28},{4,0},{8,4},{12,8},{16,12},{20,16},{24,20},{28,24},{1,29},{... | collective-permute-start | bytes 786440 | tf_op jit(solution)/shard_map/ppermute | solution.py:18
  47.1 10.7 %collective-permute-start.6 = (bf16[64,2048]{1,0:T(8,128)(2,1)S(1)}, bf16[64,2048]{1,0:T(8,128)(2,1)S(1)}, u32[]{:S(2)}, u32[]{:S(2)}) collective-permute-start(bf16[64,2048]{1,0:T(8,128)(2,1)S(1)} %collective-permute-done.4), channel_id=1, source_target_pairs={{0,4},{4,8},{8,12},{12,16},{16,20},{20,24},{24,28},{28,0},{1,5},{5... | collective-permute-start | bytes 786440 | tf_op jit(solution)/shard_map/ppermute | solution.py:15
  61.2 155.7 %copy-start.3 = (s32[64]{0:T(128)S(1)}, s32[64]{0:T(128)}, u32[]{:S(2)}) copy-start(s32[64]{0:T(128)} %param.11) | copy-start | bytes 772
